TPU v7x, 32 devices: a whole 2x2x4 slice. The times are simulated.
32 devices in a mesh: dp: 4 (over y, x), tensor: 8 (over z, core).
Axes of the slice: x: 2, y: 2, z: 4, core: 2. Of those that a mesh axis runs over, the one named last changes fastest.
Arguments:
- hidden_in: bfloat16 [12, 1024, 2048], P('dp', 'tensor'), may hold values from -6 to 6
- out_grad: bfloat16 [12, 1024, 2048], P('dp', 'tensor'), may hold values from -6 to 6
- buckets: int32 [1024, 1024], replicated, may hold values from 0 to 31
- gain_attn: bfloat16 [2048], replicated, may hold values from 0.099609375 to 1.8984375
- gain_ffn: bfloat16 [2048], replicated, may hold values from 0.099609375 to 1.8984375
- w_query: bfloat16 [2048, 2048], P('dp', 'tensor'), may hold values from -0.03125 to 0.03125
- w_key: bfloat16 [2048, 2048], P('dp', 'tensor'), may hold values from -0.125 to 0.125
- w_value: bfloat16 [2048, 2048], P('dp', 'tensor'), may hold values from -0.125 to 0.125
- w_out: bfloat16 [2048, 2048], P('tensor', 'dp'), may hold values from -1 to 1
- w_gate: bfloat16 [2048, 5120], P('dp', 'tensor'), may hold values from -0.125 to 0.125
- w_up: bfloat16 [2048, 5120], P('dp', 'tensor'), may hold values from -0.125 to 0.125
- w_down: bfloat16 [5120, 2048], P('tensor', 'dp'), may hold values from -0.125 to 0.125
- bias_table: bfloat16 [32, 32], P('dp', 'tensor'), may hold values from -4 to 4
Outputs:
- output: bfloat16 [12, 1024, 2048], P('dp', 'tensor')
- grad_input: bfloat16 [12, 1024, 2048], P('dp', 'tensor')
- grad_gain_attn: float32 [2048], replicated
- grad_gain_ffn: float32 [2048], replicated
- grad_query: float32 [2048, 2048], P('dp', 'tensor')
- grad_key: float32 [2048, 2048], P('dp', 'tensor')
- grad_value: float32 [2048, 2048], P('dp', 'tensor')
- grad_out: float32 [2048, 2048], P('tensor', 'dp')
- grad_gate: float32 [2048, 5120], P('dp', 'tensor')
- grad_up: float32 [2048, 5120], P('dp', 'tensor')
- grad_down: float32 [5120, 2048], P('tensor', 'dp')
- grad_bias: float32 [32, 32], P('dp', 'tensor')
Inputs may be any that keep to these rules, and one draw needn't show every extreme that they name: `buckets`: the bucket of each pair of query and key positions, the same for every sequence and head.
All inputs are finite; a program needn't handle non-finite values.
Results may differ from a plain program's by a relative error of at most 0.018.
Values may be sent and summed in bfloat16 or wider, within the bound.
No kernel may reach another device: no remote copies, remote signals or barrier semaphores. Data moves between devices by JAX's collectives and lax.ppermute only.
A program may use at most 320 MiB of HBM per device.

v0:
```python
import jax
import jax.numpy as jnp
from jax import lax
from jax.sharding import PartitionSpec as P

HD = 64
norm_eps = 1e-06
FULL_PRECISION = lax.Precision.HIGHEST


def rms_parts(seq_rows, gain_vec):
    inv_rms = lax.rsqrt(jnp.mean(seq_rows * seq_rows, axis=-1, keepdims=True) + norm_eps)
    plain_rows = seq_rows * inv_rms
    return (plain_rows, inv_rms, (plain_rows * gain_vec).astype(jnp.bfloat16))


def rms_back(grad_norm, plain_rows, inv_rms, gain_vec):
    scaled_grad = grad_norm * gain_vec
    return inv_rms * (
        scaled_grad - plain_rows * jnp.mean(scaled_grad * plain_rows, axis=-1, keepdims=True)
    )


def gelu_gate(gate_pre, up_pre):
    return jax.nn.gelu(gate_pre, approximate=True) * up_pre


def contract_rows(left_mat, right_mat):
    return lax.dot_general(
        left_mat, right_mat, (((0,), (0,)), ((), ())), preferred_element_type=jnp.float32
    )


def times_transpose(left_mat, right_mat):
    return lax.dot_general(
        left_mat, right_mat, (((1,), (1,)), ((), ())), preferred_element_type=jnp.float32
    )


def gather_norm(normed):
    return lax.all_gather(normed, "tensor", axis=0, tiled=True)


def gather_grad(grad_rows):
    return lax.all_gather(grad_rows, "tensor", axis=0, tiled=True)


def branch_sum(left_mat, right_mat):
    return lax.psum_scatter(
        jnp.dot(left_mat, right_mat, preferred_element_type=jnp.float32),
        "tensor",
        scatter_dimension=0,
        tiled=True,
    )


def input_sum(left_mat, right_mat):
    return lax.psum_scatter(
        times_transpose(left_mat, right_mat), "tensor", scatter_dimension=0, tiled=True
    )


def expand_bias(buckets, bias_cols):
    length = buckets.shape[0]
    block_rows = min(64, length)
    bucket_ids = jnp.arange(bias_cols.shape[0], dtype=jnp.int32)[None, :, None]

    def expand_one_block(bucket_rows):
        onehot = (bucket_rows[:, None, :] == bucket_ids).astype(jnp.float32)
        return jnp.einsum("ibj,bh->ihj", onehot, bias_cols, precision=FULL_PRECISION)

    blocks = lax.map(expand_one_block, buckets.reshape(length // block_rows, block_rows, length))
    return blocks.reshape(length, bias_cols.shape[1], length)


def bias_grad(buckets, grad_accum, bucket_count):
    length = buckets.shape[0]
    local_heads = grad_accum.shape[1]
    block_rows = min(64, length)
    bucket_ids = jnp.arange(bucket_count, dtype=jnp.int32)[None, :, None]

    def bias_one_block(carried, block_pair):
        bucket_rows, grad_rows = block_pair
        onehot = (bucket_rows[:, None, :] == bucket_ids).astype(jnp.float32)
        return (
            carried + jnp.einsum("ibj,ihj->bh", onehot, grad_rows, precision=FULL_PRECISION),
            None,
        )

    stacked = (
        buckets.reshape(length // block_rows, block_rows, length),
        grad_accum.reshape(length // block_rows, block_rows, local_heads, length),
    )
    total, _ = lax.scan(
        bias_one_block, jnp.zeros((bucket_count, local_heads), jnp.float32), stacked
    )
    return total


def body(
    hidden_in,
    out_grad,
    buckets,
    gain_attn,
    gain_ffn,
    w_query,
    w_key,
    w_value,
    w_out,
    w_gate,
    w_up,
    w_down,
    bias_table,
):
    query_cols, key_cols, value_cols, out_rows, gate_cols, up_cols, down_rows, bias_cols = (
        lax.all_gather(w_query, "dp", axis=0, tiled=True),
        lax.all_gather(w_key, "dp", axis=0, tiled=True),
        lax.all_gather(w_value, "dp", axis=0, tiled=True),
        lax.all_gather(w_out, "dp", axis=1, tiled=True),
        lax.all_gather(w_gate, "dp", axis=0, tiled=True),
        lax.all_gather(w_up, "dp", axis=0, tiled=True),
        lax.all_gather(w_down, "dp", axis=1, tiled=True),
        lax.all_gather(bias_table, "dp", axis=0, tiled=True),
    )
    gain_one = gain_attn.astype(jnp.float32)
    gain_two = gain_ffn.astype(jnp.float32)
    w_qkv = jnp.concatenate([query_cols, key_cols, value_cols], axis=1)
    w_ffn = jnp.concatenate([gate_cols, up_cols], axis=1)
    local_inner = query_cols.shape[1]
    local_heads = local_inner // HD
    local_ff = gate_cols.shape[1]
    seq_len = buckets.shape[0]
    model_dim = hidden_in.shape[2]
    block_len = min(512, seq_len)
    block_starts = list(range(0, seq_len, block_len))
    bias_full = expand_bias(buckets, bias_cols.astype(jnp.float32))
    out_initial = jnp.zeros((local_inner, model_dim), jnp.float32)

    def block_scores(queries, key_rows, row_start):
        query_block = queries[row_start : row_start + block_len]
        scores = jnp.einsum(
            "ihd,jhd->ihj", query_block, key_rows, preferred_element_type=jnp.float32
        )
        return (query_block, scores + bias_full[row_start : row_start + block_len])

    def micro_step(carried, scan_pair):
        grad_qkv, grad_outw, grad_ffn, grad_downw, grad_gone, grad_gtwo, grad_table = carried
        seq_in, seq_cot = scan_pair
        seq_rows = seq_in.astype(jnp.float32)
        plain_one, inv_one, norm_one = rms_parts(seq_rows, gain_one)
        norm_full = gather_norm(norm_one)
        projected = jnp.dot(norm_full, w_qkv, preferred_element_type=jnp.float32).astype(
            jnp.bfloat16
        )
        queries = projected[:, :local_inner].reshape(seq_len, local_heads, HD)
        key_rows = projected[:, local_inner : 2 * local_inner].reshape(seq_len, local_heads, HD)
        value_rows = projected[:, 2 * local_inner :].reshape(seq_len, local_heads, HD)
        context_parts = []
        lse_parts = []
        for row_start in block_starts:
            query_block, scores = block_scores(queries, key_rows, row_start)
            top_score = jnp.max(scores, axis=-1, keepdims=True)
            shifted = jnp.exp(scores - top_score)
            totals = jnp.sum(shifted, axis=-1, keepdims=True)
            attn_probs = shifted / totals
            lse_parts.append(top_score + jnp.log(totals))
            context_parts.append(
                jnp.einsum(
                    "ihj,jhd->ihd",
                    attn_probs.astype(jnp.bfloat16),
                    value_rows,
                    preferred_element_type=jnp.float32,
                ).astype(jnp.bfloat16)
            )
        context = jnp.concatenate(context_parts, axis=0).reshape(seq_len, local_inner)
        attn_rows = branch_sum(context, out_rows)
        mid_rows = seq_rows + attn_rows
        plain_two, inv_two, norm_two = rms_parts(mid_rows, gain_two)
        norm_full_two = gather_norm(norm_two)
        pre_ffn = jnp.dot(norm_full_two, w_ffn, preferred_element_type=jnp.float32)
        gate_pre = pre_ffn[:, :local_ff]
        up_pre = pre_ffn[:, local_ff:]
        hidden = gelu_gate(gate_pre, up_pre).astype(jnp.bfloat16)
        ffn_rows = branch_sum(hidden, down_rows)
        seq_out = (mid_rows + ffn_rows).astype(jnp.bfloat16)
        cot_full = gather_grad(seq_cot)
        grad_downw = grad_downw + contract_rows(hidden, cot_full)
        grad_hidden = times_transpose(cot_full, down_rows)
        _, gelu_pull = jax.vjp(gelu_gate, gate_pre, up_pre)
        grad_gate_pre, grad_up_pre = gelu_pull(grad_hidden)
        grad_pre = jnp.concatenate([grad_gate_pre, grad_up_pre], axis=1).astype(jnp.bfloat16)
        grad_ffn = grad_ffn + contract_rows(norm_full_two, grad_pre)
        grad_norm_two = input_sum(grad_pre, w_ffn)
        grad_gtwo = grad_gtwo + jnp.sum(grad_norm_two * plain_two, axis=0)
        grad_mid = seq_cot.astype(jnp.float32) + rms_back(
            grad_norm_two, plain_two, inv_two, gain_two
        )
        grad_mid_low = grad_mid.astype(jnp.bfloat16)
        grad_full = gather_grad(grad_mid_low)
        grad_context = times_transpose(grad_full, out_rows).astype(jnp.bfloat16)
        grad_outw = grad_outw + contract_rows(context, grad_full)
        grad_context = grad_context.reshape(seq_len, local_heads, HD)
        grad_query_parts = []
        grad_keys = jnp.zeros((seq_len, local_heads, HD), jnp.float32)
        grad_values = jnp.zeros((seq_len, local_heads, HD), jnp.float32)
        for block_index, row_start in enumerate(block_starts):
            query_block, scores = block_scores(queries, key_rows, row_start)
            attn_probs = jnp.exp(scores - lse_parts[block_index])
            probs_low = attn_probs.astype(jnp.bfloat16)
            grad_block = grad_context[row_start : row_start + block_len]
            grad_probs = jnp.einsum(
                "ihd,jhd->ihj", grad_block, value_rows, preferred_element_type=jnp.float32
            )
            row_inner = jnp.sum(attn_probs * grad_probs, axis=-1, keepdims=True)
            grad_scores = (attn_probs * (grad_probs - row_inner)).astype(jnp.bfloat16)
            grad_table = grad_table.at[row_start : row_start + block_len].add(
                grad_scores.astype(jnp.float32)
            )
            grad_query_parts.append(
                jnp.einsum(
                    "ihj,jhd->ihd", grad_scores, key_rows, preferred_element_type=jnp.float32
                )
            )
            grad_keys = grad_keys + jnp.einsum(
                "ihj,ihd->jhd", grad_scores, query_block, preferred_element_type=jnp.float32
            )
            grad_values = grad_values + jnp.einsum(
                "ihj,ihd->jhd", probs_low, grad_block, preferred_element_type=jnp.float32
            )
        grad_queries = jnp.concatenate(grad_query_parts, axis=0)
        grad_proj = jnp.concatenate(
            [
                grad_queries.reshape(seq_len, local_inner),
                grad_keys.reshape(seq_len, local_inner),
                grad_values.reshape(seq_len, local_inner),
            ],
            axis=1,
        ).astype(jnp.bfloat16)
        grad_qkv = grad_qkv + contract_rows(norm_full, grad_proj)
        grad_norm_one = input_sum(grad_proj, w_qkv)
        grad_gone = grad_gone + jnp.sum(grad_norm_one * plain_one, axis=0)
        grad_in = (grad_mid + rms_back(grad_norm_one, plain_one, inv_one, gain_one)).astype(
            jnp.bfloat16
        )
        new_carry = (grad_qkv, grad_outw, grad_ffn, grad_downw, grad_gone, grad_gtwo, grad_table)
        return (new_carry, (seq_out, grad_in))

    initial = (
        jnp.zeros((model_dim, 3 * local_inner), jnp.float32),
        out_initial,
        jnp.zeros((model_dim, 2 * local_ff), jnp.float32),
        jnp.zeros((local_ff, model_dim), jnp.float32),
        jnp.zeros((model_dim,), jnp.float32),
        jnp.zeros((model_dim,), jnp.float32),
        jnp.zeros((seq_len, local_heads, seq_len), jnp.float32),
    )
    final_carry, (outputs_seq, grads_seq) = lax.scan(micro_step, initial, (hidden_in, out_grad))
    grad_qkv, grad_outw, grad_ffn, grad_downw, grad_gone, grad_gtwo, grad_table = final_carry
    table_grad = bias_grad(buckets, grad_table, bias_cols.shape[0])
    shards = (
        lax.psum_scatter(
            grad_qkv[:, :local_inner].astype(jnp.bfloat16), "dp", scatter_dimension=0, tiled=True
        ).astype(jnp.float32),
        lax.psum_scatter(
            grad_qkv[:, local_inner : 2 * local_inner].astype(jnp.bfloat16),
            "dp",
            scatter_dimension=0,
            tiled=True,
        ).astype(jnp.float32),
        lax.psum_scatter(
            grad_qkv[:, 2 * local_inner :].astype(jnp.bfloat16),
            "dp",
            scatter_dimension=0,
            tiled=True,
        ).astype(jnp.float32),
        lax.psum_scatter(
            grad_outw.astype(jnp.bfloat16), "dp", scatter_dimension=1, tiled=True
        ).astype(jnp.float32),
        lax.psum_scatter(
            grad_ffn[:, :local_ff].astype(jnp.bfloat16), "dp", scatter_dimension=0, tiled=True
        ).astype(jnp.float32),
        lax.psum_scatter(
            grad_ffn[:, local_ff:].astype(jnp.bfloat16), "dp", scatter_dimension=0, tiled=True
        ).astype(jnp.float32),
        lax.psum_scatter(
            grad_downw.astype(jnp.bfloat16), "dp", scatter_dimension=1, tiled=True
        ).astype(jnp.float32),
        lax.psum_scatter(
            table_grad.astype(jnp.bfloat16), "dp", scatter_dimension=0, tiled=True
        ).astype(jnp.float32),
    )
    gain_sums = lax.psum((grad_gone, grad_gtwo), ("dp", "tensor"))
    return (
        outputs_seq,
        grads_seq,
        gain_sums[0],
        gain_sums[1],
        shards[0],
        shards[1],
        shards[2],
        shards[3],
        shards[4],
        shards[5],
        shards[6],
        shards[7],
    )


def solution(mesh):
    in_specs = (
        P("dp", "tensor", None),
        P("dp", "tensor", None),
        P(),
        P(),
        P(),
        P("dp", "tensor"),
        P("dp", "tensor"),
        P("dp", "tensor"),
        P("tensor", "dp"),
        P("dp", "tensor"),
        P("dp", "tensor"),
        P("tensor", "dp"),
        P("dp", "tensor"),
    )
    out_specs = (
        P("dp", "tensor", None),
        P("dp", "tensor", None),
        P(),
        P(),
        P("dp", "tensor"),
        P("dp", "tensor"),
        P("dp", "tensor"),
        P("tensor", "dp"),
        P("dp", "tensor"),
        P("dp", "tensor"),
        P("tensor", "dp"),
        P("dp", "tensor"),
    )
    return jax.shard_map(body, mesh=mesh, in_specs=in_specs, out_specs=out_specs, check_vma=False)
```

profile of v0, /device:TPU:0, one launch (start us, length us, event | category | flops | bytes accessed | tf_op | source)
XLA Modules:
  0.0 2525.8 jit_solution(10109821729811257224)
XLA Ops:
  21.7 73.3 %while.53 = (s32[]{:T(128)}, f32[16,64,4,1024]{3,2,1,0:T(4,128)}, s32[16,64,1024]{2,1,0:T(8,128)}, f32[32,4]{0,1:T(4,128)S(1)}, s32[]{:T(128)}) while((s32[]{:T(128)}, f32[16,64,4,1024]{3,2,1,0:T(4,128)}, s32[16,64,1024]{2,1,0:T(8,128)}, f32[32,4]{0,1:T(4,128)S(1)}, s32[]{:T(128)}) %tuple.177), condition=%wide.region_1.2_spmd.clone, body=%wide.region_0.1_spmd.clone.sunk | while | flops 102760448 | bytes 1835597 | solution.py:72
  95.1 19.3 copy.64
  117.5 19.6 all-gather.27.cloned.1.call-done
  137.1 41.2 %all-gather.29.cloned.1.call-done = bf16[2048,640]{1,0:T(8,128)(2,1)} async-done(((bf16[512,640]{1,0:T(8,128)(2,1)}), bf16[2048,640]{1,0:T(8,128)(2,1)}) %all-gather.29.cloned.1.call-update) | async-done | bytes 2621456 | tf_op jit(solution)/shard_map/all_gather | solution.py:121
  183.6 22.7 all-gather.23.cloned.1.call-done
  206.4 41.2 %all-gather.25.cloned.1.call-done = bf16[640,2048]{1,0:T(8,128)(2,1)} async-done(((bf16[640,512]{1,0:T(8,128)(2,1)}), bf16[640,2048]{1,0:T(8,128)(2,1)}) %all-gather.25.cloned.1.call-update) | async-done | bytes 2621456 | tf_op jit(solution)/shard_map/all_gather | solution.py:122
  255.5 2008.2 %while.54 = (s32[]{:T(128)}, f32[2048,768]{1,0:T(8,128)}, f32[256,2048]{1,0:T(8,128)}, f32[2048,1280]{1,0:T(8,128)}, f32[640,2048]{1,0:T(8,128)}, /*index=5*/f32...) while((s32[]{:T(128)}, f32[2048,768]{1,0:T(8,128)}, ...), condition=%wide.region_19.20_spmd.clone, body=%wide.region_2.19_spmd.clone.sunk | while | flops 40408182784 | bytes 830275520 | solution.py:257
  258.9 47.0 %all-gather.31.cloned.1.call-done = bf16[1024,2048]{1,0:T(8,128)(2,1)} async-done(((bf16[128,2048]{1,0:T(8,128)(2,1)}), bf16[1024,2048]{1,0:T(8,128)(2,1)}) %all-gather.31.cloned.1.call-update) | async-done | bytes 4194320 | tf_op jit(solution)/shard_map/while/body/eval_jaxpr/all_gather | solution.py:41
  336.9 88.4 %reduce-scatter.27.cloned.1.call-done = f32[128,2048]{1,0:T(8,128)} async-done(((f32[1024,2048]{1,0:T(8,128)}), f32[128,2048]{1,0:T(8,128)}) %reduce-scatter.27.cloned.1.call-update) | async-done | bytes 1048592 | tf_op jit(solution)/shard_map/while/body/eval_jaxpr/reduce_scatter | solution.py:49
  429.9 43.5 %all-gather.33.cloned.1.call-done = bf16[1024,2048]{1,0:T(8,128)(2,1)} async-done(((bf16[128,2048]{1,0:T(8,128)(2,1)}), bf16[1024,2048]{1,0:T(8,128)(2,1)}) %all-gather.33.cloned.1.call-update) | async-done | bytes 4194320 | tf_op jit(solution)/shard_map/while/body/eval_jaxpr/all_gather | solution.py:41
  473.4 10.3 fusion.263
  483.7 37.6 %all-gather.35.cloned.1.call-done = bf16[1,1024,2048]{2,1,0:T(8,128)(2,1)} async-done(((bf16[1,128,2048]{2,1,0:T(8,128)(2,1)}), bf16[1,1024,2048]{2,1,0:T(8,128)(2,1)}) %all-gather.35.cloned.1.call-update) | async-done | bytes 4194320 | tf_op jit(solution)/shard_map/while/body/eval_jaxpr/all_gather | solution.py:45
  521.2 10.4 fusion.264
  533.1 10.4 fusion.265
  543.5 88.5 %reduce-scatter.29.cloned.1.call-done = f32[128,2048]{1,0:T(8,128)} async-done(((f32[1024,2048]{1,0:T(8,128)}), f32[128,2048]{1,0:T(8,128)}) %reduce-scatter.29.cloned.1.call-update) | async-done | bytes 1048592 | tf_op jit(solution)/shard_map/while/body/eval_jaxpr/reduce_scatter | solution.py:58
  637.0 45.2 %all-gather.37.cloned.1.call-done = bf16[1024,2048]{1,0:T(8,128)(2,1)} async-done(((bf16[128,2048]{1,0:T(8,128)(2,1)}), bf16[1024,2048]{1,0:T(8,128)(2,1)}) %all-gather.37.cloned.1.call-update) | async-done | bytes 4194320 | tf_op jit(solution)/shard_map/while/body/eval_jaxpr/all_gather | solution.py:45
  695.9 10.3 add_dynamic-update-slice_fusion.2
  776.3 53.9 %reduce-scatter.31.cloned.1.call-done = f32[128,2048]{1,0:T(8,128)} async-done(((f32[1024,2048]{1,0:T(8,128)}), f32[128,2048]{1,0:T(8,128)}) %reduce-scatter.31.cloned.1.call-update) | async-done | bytes 1048592 | tf_op jit(solution)/shard_map/while/body/eval_jaxpr/reduce_scatter | solution.py:58
  831.9 88.4 %reduce-scatter.33.cloned.1.call-done = f32[128,2048]{1,0:T(8,128)} async-done(((f32[1024,2048]{1,0:T(8,128)}), f32[128,2048]{1,0:T(8,128)}) %reduce-scatter.33.cloned.1.call-update) | async-done | bytes 1048592 | tf_op jit(solution)/shard_map/while/body/eval_jaxpr/reduce_scatter | solution.py:49
  927.3 45.4 %all-gather.31.cloned.1.call-done = bf16[1024,2048]{1,0:T(8,128)(2,1)} async-done(((bf16[128,2048]{1,0:T(8,128)(2,1)}), bf16[1024,2048]{1,0:T(8,128)(2,1)}) %all-gather.31.cloned.1.call-update) | async-done | bytes 4194320 | tf_op jit(solution)/shard_map/while/body/eval_jaxpr/all_gather | solution.py:41
  1003.7 88.4 %reduce-scatter.27.cloned.1.call-done = f32[128,2048]{1,0:T(8,128)} async-done(((f32[1024,2048]{1,0:T(8,128)}), f32[128,2048]{1,0:T(8,128)}) %reduce-scatter.27.cloned.1.call-update) | async-done | bytes 1048592 | tf_op jit(solution)/shard_map/while/body/eval_jaxpr/reduce_scatter | solution.py:49
  1096.8 43.5 %all-gather.33.cloned.1.call-done = bf16[1024,2048]{1,0:T(8,128)(2,1)} async-done(((bf16[128,2048]{1,0:T(8,128)(2,1)}), bf16[1024,2048]{1,0:T(8,128)(2,1)}) %all-gather.33.cloned.1.call-update) | async-done | bytes 4194320 | tf_op jit(solution)/shard_map/while/body/eval_jaxpr/all_gather | solution.py:41
  1150.6 37.6 %all-gather.35.cloned.1.call-done = bf16[1,1024,2048]{2,1,0:T(8,128)(2,1)} async-done(((bf16[1,128,2048]{2,1,0:T(8,128)(2,1)}), bf16[1,1024,2048]{2,1,0:T(8,128)(2,1)}) %all-gather.35.cloned.1.call-update) | async-done | bytes 4194320 | tf_op jit(solution)/shard_map/while/body/eval_jaxpr/all_gather | solution.py:45
  1188.1 10.4 fusion.264
  1200.0 10.4 fusion.265
  1210.4 88.4 %reduce-scatter.29.cloned.1.call-done = f32[128,2048]{1,0:T(8,128)} async-done(((f32[1024,2048]{1,0:T(8,128)}), f32[128,2048]{1,0:T(8,128)}) %reduce-scatter.29.cloned.1.call-update) | async-done | bytes 1048592 | tf_op jit(solution)/shard_map/while/body/eval_jaxpr/reduce_scatter | solution.py:58
  1303.8 45.2 %all-gather.37.cloned.1.call-done = bf16[1024,2048]{1,0:T(8,128)(2,1)} async-done(((bf16[128,2048]{1,0:T(8,128)(2,1)}), bf16[1024,2048]{1,0:T(8,128)(2,1)}) %all-gather.37.cloned.1.call-update) | async-done | bytes 4194320 | tf_op jit(solution)/shard_map/while/body/eval_jaxpr/all_gather | solution.py:45
  1362.8 10.3 add_dynamic-update-slice_fusion.2
  1427.3 11.5 select_add_fusion.11
  1449.5 47.5 %reduce-scatter.31.cloned.1.call-done = f32[128,2048]{1,0:T(8,128)} async-done(((f32[1024,2048]{1,0:T(8,128)}), f32[128,2048]{1,0:T(8,128)}) %reduce-scatter.31.cloned.1.call-update) | async-done | bytes 1048592 | tf_op jit(solution)/shard_map/while/body/eval_jaxpr/reduce_scatter | solution.py:58
  1498.8 88.5 %reduce-scatter.33.cloned.1.call-done = f32[128,2048]{1,0:T(8,128)} async-done(((f32[1024,2048]{1,0:T(8,128)}), f32[128,2048]{1,0:T(8,128)}) %reduce-scatter.33.cloned.1.call-update) | async-done | bytes 1048592 | tf_op jit(solution)/shard_map/while/body/eval_jaxpr/reduce_scatter | solution.py:49
  1594.3 45.4 %all-gather.31.cloned.1.call-done = bf16[1024,2048]{1,0:T(8,128)(2,1)} async-done(((bf16[128,2048]{1,0:T(8,128)(2,1)}), bf16[1024,2048]{1,0:T(8,128)(2,1)}) %all-gather.31.cloned.1.call-update) | async-done | bytes 4194320 | tf_op jit(solution)/shard_map/while/body/eval_jaxpr/all_gather | solution.py:41
  1670.8 88.4 %reduce-scatter.27.cloned.1.call-done = f32[128,2048]{1,0:T(8,128)} async-done(((f32[1024,2048]{1,0:T(8,128)}), f32[128,2048]{1,0:T(8,128)}) %reduce-scatter.27.cloned.1.call-update) | async-done | bytes 1048592 | tf_op jit(solution)/shard_map/while/body/eval_jaxpr/reduce_scatter | solution.py:49
  1763.8 43.5 %all-gather.33.cloned.1.call-done = bf16[1024,2048]{1,0:T(8,128)(2,1)} async-done(((bf16[128,2048]{1,0:T(8,128)(2,1)}), bf16[1024,2048]{1,0:T(8,128)(2,1)}) %all-gather.33.cloned.1.call-update) | async-done | bytes 4194320 | tf_op jit(solution)/shard_map/while/body/eval_jaxpr/all_gather | solution.py:41
  1807.3 10.3 fusion.263
  1817.6 37.4 %all-gather.35.cloned.1.call-done = bf16[1,1024,2048]{2,1,0:T(8,128)(2,1)} async-done(((bf16[1,128,2048]{2,1,0:T(8,128)(2,1)}), bf16[1,1024,2048]{2,1,0:T(8,128)(2,1)}) %all-gather.35.cloned.1.call-update) | async-done | bytes 4194320 | tf_op jit(solution)/shard_map/while/body/eval_jaxpr/all_gather | solution.py:45
  1855.0 10.4 fusion.264
  1866.8 10.4 fusion.265
  1877.3 88.4 %reduce-scatter.29.cloned.1.call-done = f32[128,2048]{1,0:T(8,128)} async-done(((f32[1024,2048]{1,0:T(8,128)}), f32[128,2048]{1,0:T(8,128)}) %reduce-scatter.29.cloned.1.call-update) | async-done | bytes 1048592 | tf_op jit(solution)/shard_map/while/body/eval_jaxpr/reduce_scatter | solution.py:58
  1970.7 45.2 %all-gather.37.cloned.1.call-done = bf16[1024,2048]{1,0:T(8,128)(2,1)} async-done(((bf16[128,2048]{1,0:T(8,128)(2,1)}), bf16[1024,2048]{1,0:T(8,128)(2,1)}) %all-gather.37.cloned.1.call-update) | async-done | bytes 4194320 | tf_op jit(solution)/shard_map/while/body/eval_jaxpr/all_gather | solution.py:45
  2029.7 10.3 add_dynamic-update-slice_fusion.2
  2094.2 11.5 select_add_fusion.11
  2116.3 47.5 %reduce-scatter.31.cloned.1.call-done = f32[128,2048]{1,0:T(8,128)} async-done(((f32[1024,2048]{1,0:T(8,128)}), f32[128,2048]{1,0:T(8,128)}) %reduce-scatter.31.cloned.1.call-update) | async-done | bytes 1048592 | tf_op jit(solution)/shard_map/while/body/eval_jaxpr/reduce_scatter | solution.py:58
  2165.6 88.6 %reduce-scatter.33.cloned.1.call-done = f32[128,2048]{1,0:T(8,128)} async-done(((f32[1024,2048]{1,0:T(8,128)}), f32[128,2048]{1,0:T(8,128)}) %reduce-scatter.33.cloned.1.call-update) | async-done | bytes 1048592 | tf_op jit(solution)/shard_map/while/body/eval_jaxpr/reduce_scatter | solution.py:49
  2286.2 20.2 copy.65
  2306.5 104.5 %while.55 = (s32[]{:T(128)}, f32[32,4]{0,1:T(4,128)S(1)}, s32[16,64,1024]{2,1,0:T(8,128)}, f32[16,64,4,1024]{3,2,1,0:T(4,128)}, s32[]{:T(128)}, /*index=5*/s32[]{:T(128)}) while((s32[]{:T(128)}, f32[32,4]{0,1:T(4,128)S(1)}, s32[16,64,1024]{2,1,0:T(8,128)}, f32[16,64,4,1024]{3,2,1,0:T(4,128)}, s32[]{:T(128)}, ...), condition=%wide.region_30.31_spmd.clone, body=%wide.region_29.30_spmd.clone.sunk | while | flops 102760704 | bytes 1836127 | solution.py:94
  2420.8 37.9 %all-reduce.1 = (f32[2048]{0:T(1024)}, f32[2048]{0:T(1024)}) all-reduce(f32[2048]{0:T(1024)S(1)} %copy-done.26, f32[2048]{0:T(1024)S(1)} %copy-done.23), channel_id=1, replica_groups=mesh['dp'=4,'tensor'=8] {'dp','tensor'}, use_global_device_ids=true, to_apply=%region_20.21 | all-reduce | flops 4096 | bytes 32768 | tf_op jit(solution)/shard_map/psum | solution.py:292
  2476.4 40.4 %reduce-scatter.23.cloned.1.call-done = bf16[512,640]{1,0:T(8,128)(2,1)} async-done(((bf16[2048,640]{1,0:T(8,128)(2,1)}), bf16[512,640]{1,0:T(8,128)(2,1)}) %reduce-scatter.23.cloned.1.call-update) | async-done | bytes 655376 | tf_op jit(solution)/shard_map/reduce_scatter | solution.py:282
  (583 shorter events, 661.5 us)
Async XLA Ops:
  7.2 107.2 %all-gather.17.cloned.1.call-start = ((), (), s32[]{:S(2)}) async-start(), calls=%async_computation.11 | async-start | bytes 1310720 | tf_op jit(solution)/shard_map/all_gather | solution.py:116
  7.9 106.5 %all-gather.19.cloned.1.call-start = ((), (), s32[]{:S(2)}) async-start(), calls=%async_computation.12 | async-start | bytes 1310720 | tf_op jit(solution)/shard_map/all_gather | solution.py:117
  8.7 105.7 %all-gather.21.cloned.1.call-start = ((), (), s32[]{:S(2)}) async-start(), calls=%async_computation.13 | async-start | bytes 1310720 | tf_op jit(solution)/shard_map/all_gather | solution.py:118
  9.4 127.7 %all-gather.27.cloned.1.call-start = ((), (), s32[]{:S(2)}) async-start(), calls=%async_computation.16 | async-start | bytes 3276800 | tf_op jit(solution)/shard_map/all_gather | solution.py:120
  10.0 168.3 %all-gather.29.cloned.1.call-start = ((), (), s32[]{:S(2)}) async-start(), calls=%async_computation.17 | async-start | bytes 3276800 | tf_op jit(solution)/shard_map/all_gather | solution.py:121
  10.6 195.8 %all-gather.23.cloned.1.call-start = ((), (), s32[]{:S(2)}) async-start(), calls=%async_computation.14 | async-start | bytes 1310720 | tf_op jit(solution)/shard_map/all_gather | solution.py:119
  11.1 236.5 %all-gather.25.cloned.1.call-start = ((), (), s32[]{:S(2)}) async-start(), calls=%async_computation.15 | async-start | bytes 3276800 | tf_op jit(solution)/shard_map/all_gather | solution.py:122
  255.5 50.3 %all-gather.31.cloned.1.call-start = ((), (), s32[]{:S(2)}) async-start(), calls=%async_computation.25 | async-start | bytes 4718592 | tf_op jit(solution)/shard_map/while/body/eval_jaxpr/all_gather | solution.py:41
  258.8 166.5 %reduce-scatter.27.cloned.1.call-start = ((), (), s32[]{:S(2)}) async-start(), calls=%async_computation.26 | async-start | bytes 9437184 | tf_op jit(solution)/shard_map/while/body/eval_jaxpr/reduce_scatter | solution.py:49
  336.8 136.5 %all-gather.33.cloned.1.call-start = ((), (), s32[]{:S(2)}) async-start(), calls=%async_computation.27 | async-start | bytes 4718592 | tf_op jit(solution)/shard_map/while/body/eval_jaxpr/all_gather | solution.py:41
  426.9 207.3 %copy-start.27 = (f32[128]{0:T(128)}, f32[128]{0:T(128)S(1)}, u32[]{:S(2)}) copy-start(f32[128]{0:T(128)S(1)} %add_rsqrt_fusion.5) | copy-start | bytes 1540 | tf_op jit(solution)/shard_map/while
  427.9 93.4 %all-gather.35.cloned.1.call-start = ((), (), s32[]{:S(2)}) async-start(), calls=%async_computation.28 | async-start | bytes 4718592 | tf_op jit(solution)/shard_map/while/body/eval_jaxpr/all_gather | solution.py:45
  429.8 202.2 %reduce-scatter.29.cloned.1.call-start = ((), (), s32[]{:S(2)}) async-start(), calls=%async_computation.29 | async-start | bytes 9437184 | tf_op jit(solution)/shard_map/while/body/eval_jaxpr/reduce_scatter | solution.py:58
  543.5 138.7 %all-gather.37.cloned.1.call-start = ((), (), s32[]{:S(2)}) async-start(), calls=%async_computation.30 | async-start | bytes 4718592 | tf_op jit(solution)/shard_map/while/body/eval_jaxpr/all_gather | solution.py:45
  636.7 193.4 %reduce-scatter.31.cloned.1.call-start = ((), (), s32[]{:S(2)}) async-start(), calls=%async_computation.31 | async-start | bytes 9437184 | tf_op jit(solution)/shard_map/while/body/eval_jaxpr/reduce_scatter | solution.py:58
  741.6 178.7 %reduce-scatter.33.cloned.1.call-start = ((), (), s32[]{:S(2)}) async-start(), calls=%async_computation.32 | async-start | bytes 9437184 | tf_op jit(solution)/shard_map/while/body/eval_jaxpr/reduce_scatter | solution.py:49
  770.7 149.6 %copy-start.3 = (f32[128,2048]{1,0:T(8,128)S(1)}, f32[128,2048]{1,0:T(8,128)}, u32[]{:S(2)}) copy-start(f32[128,2048]{1,0:T(8,128)} %reduce-scatter.29.cloned.1.call-done) | copy-start | bytes 3145732 | tf_op jit(solution)/shard_map/while
  770.7 149.6 %copy-start.28 = (f32[128]{0:T(128)S(1)}, f32[128]{0:T(128)}, u32[]{:S(2)}) copy-start(f32[128]{0:T(128)} %copy-done.27) | copy-start | bytes 1540 | tf_op jit(solution)/shard_map/while
  770.7 149.5 %copy-start.32 = (f32[128]{0:T(128)S(1)}, f32[128]{0:T(128)}, u32[]{:S(2)}) copy-start(f32[128]{0:T(128)} %copy-done.31) | copy-start | bytes 1540 | tf_op jit(solution)/shard_map/while
  776.2 147.4 %copy-start.19 = (f32[2048]{0:T(1024)S(1)}, f32[2048]{0:T(1024)}, u32[]{:S(2)}) copy-start(f32[2048]{0:T(1024)} %copy-done.18) | copy-start | bytes 24580 | tf_op jit(solution)/shard_map/while
  923.9 48.8 %all-gather.31.cloned.1.call-start = ((), (), s32[]{:S(2)}) async-start(), calls=%async_computation.25 | async-start | bytes 4718592 | tf_op jit(solution)/shard_map/while/body/eval_jaxpr/all_gather | solution.py:41
  927.2 164.9 %reduce-scatter.27.cloned.1.call-start = ((), (), s32[]{:S(2)}) async-start(), calls=%async_computation.26 | async-start | bytes 9437184 | tf_op jit(solution)/shard_map/while/body/eval_jaxpr/reduce_scatter | solution.py:49
  1003.7 136.6 %all-gather.33.cloned.1.call-start = ((), (), s32[]{:S(2)}) async-start(), calls=%async_computation.27 | async-start | bytes 4718592 | tf_op jit(solution)/shard_map/while/body/eval_jaxpr/all_gather | solution.py:41
  1093.8 207.3 %copy-start.27 = (f32[128]{0:T(128)}, f32[128]{0:T(128)S(1)}, u32[]{:S(2)}) copy-start(f32[128]{0:T(128)S(1)} %add_rsqrt_fusion.5) | copy-start | bytes 1540 | tf_op jit(solution)/shard_map/while
  1094.7 93.4 %all-gather.35.cloned.1.call-start = ((), (), s32[]{:S(2)}) async-start(), calls=%async_computation.28 | async-start | bytes 4718592 | tf_op jit(solution)/shard_map/while/body/eval_jaxpr/all_gather | solution.py:45
  1096.7 202.2 %reduce-scatter.29.cloned.1.call-start = ((), (), s32[]{:S(2)}) async-start(), calls=%async_computation.29 | async-start | bytes 9437184 | tf_op jit(solution)/shard_map/while/body/eval_jaxpr/reduce_scatter | solution.py:58
  1210.4 138.7 %all-gather.37.cloned.1.call-start = ((), (), s32[]{:S(2)}) async-start(), calls=%async_computation.30 | async-start | bytes 4718592 | tf_op jit(solution)/shard_map/while/body/eval_jaxpr/all_gather | solution.py:45
  1303.6 193.4 %reduce-scatter.31.cloned.1.call-start = ((), (), s32[]{:S(2)}) async-start(), calls=%async_computation.31 | async-start | bytes 9437184 | tf_op jit(solution)/shard_map/while/body/eval_jaxpr/reduce_scatter | solution.py:58
  1408.5 178.8 %reduce-scatter.33.cloned.1.call-start = ((), (), s32[]{:S(2)}) async-start(), calls=%async_computation.32 | async-start | bytes 9437184 | tf_op jit(solution)/shard_map/while/body/eval_jaxpr/reduce_scatter | solution.py:49
  1590.9 48.8 %all-gather.31.cloned.1.call-start = ((), (), s32[]{:S(2)}) async-start(), calls=%async_computation.25 | async-start | bytes 4718592 | tf_op jit(solution)/shard_map/while/body/eval_jaxpr/all_gather | solution.py:41
  1594.2 164.9 %reduce-scatter.27.cloned.1.call-start = ((), (), s32[]{:S(2)}) async-start(), calls=%async_computation.26 | async-start | bytes 9437184 | tf_op jit(solution)/shard_map/while/body/eval_jaxpr/reduce_scatter | solution.py:49
  1670.7 136.5 %all-gather.33.cloned.1.call-start = ((), (), s32[]{:S(2)}) async-start(), calls=%async_computation.27 | async-start | bytes 4718592 | tf_op jit(solution)/shard_map/while/body/eval_jaxpr/all_gather | solution.py:41
  1760.8 207.1 %copy-start.27 = (f32[128]{0:T(128)}, f32[128]{0:T(128)S(1)}, u32[]{:S(2)}) copy-start(f32[128]{0:T(128)S(1)} %add_rsqrt_fusion.5) | copy-start | bytes 1540 | tf_op jit(solution)/shard_map/while
  1761.8 93.2 %all-gather.35.cloned.1.call-start = ((), (), s32[]{:S(2)}) async-start(), calls=%async_computation.28 | async-start | bytes 4718592 | tf_op jit(solution)/shard_map/while/body/eval_jaxpr/all_gather | solution.py:45
  1763.7 202.0 %reduce-scatter.29.cloned.1.call-start = ((), (), s32[]{:S(2)}) async-start(), calls=%async_computation.29 | async-start | bytes 9437184 | tf_op jit(solution)/shard_map/while/body/eval_jaxpr/reduce_scatter | solution.py:58
  1877.2 138.7 %all-gather.37.cloned.1.call-start = ((), (), s32[]{:S(2)}) async-start(), calls=%async_computation.30 | async-start | bytes 4718592 | tf_op jit(solution)/shard_map/while/body/eval_jaxpr/all_gather | solution.py:45
  1970.4 193.4 %reduce-scatter.31.cloned.1.call-start = ((), (), s32[]{:S(2)}) async-start(), calls=%async_computation.31 | async-start | bytes 9437184 | tf_op jit(solution)/shard_map/while/body/eval_jaxpr/reduce_scatter | solution.py:58
  2075.3 178.8 %reduce-scatter.33.cloned.1.call-start = ((), (), s32[]{:S(2)}) async-start(), calls=%async_computation.32 | async-start | bytes 9437184 | tf_op jit(solution)/shard_map/while/body/eval_jaxpr/reduce_scatter | solution.py:49
  2108.8 145.3 %copy-start.3 = (f32[128,2048]{1,0:T(8,128)S(1)}, f32[128,2048]{1,0:T(8,128)}, u32[]{:S(2)}) copy-start(f32[128,2048]{1,0:T(8,128)} %reduce-scatter.29.cloned.1.call-done) | copy-start | bytes 3145732 | tf_op jit(solution)/shard_map/while
  2108.8 145.3 %copy-start.28 = (f32[128]{0:T(128)S(1)}, f32[128]{0:T(128)}, u32[]{:S(2)}) copy-start(f32[128]{0:T(128)} %copy-done.27) | copy-start | bytes 1540 | tf_op jit(solution)/shard_map/while
  2108.8 145.3 %copy-start.32 = (f32[128]{0:T(128)S(1)}, f32[128]{0:T(128)}, u32[]{:S(2)}) copy-start(f32[128]{0:T(128)} %copy-done.31) | copy-start | bytes 1540 | tf_op jit(solution)/shard_map/while
  2263.7 195.7 %reduce-scatter.19.cloned.1.call-start = ((), (), s32[]{:S(2)}) async-start(), calls=%async_computation.21 | async-start | bytes 1310720 | tf_op jit(solution)/shard_map/reduce_scatter | solution.py:276
  2266.5 194.7 %reduce-scatter.13.cloned.1.call-start = ((), (), s32[]{:S(2)}) async-start(), calls=%async_computation.18 | async-start | bytes 1310720 | tf_op jit(solution)/shard_map/reduce_scatter | solution.py:261
  2271.4 191.6 %reduce-scatter.15.cloned.1.call-start = ((), (), s32[]{:S(2)}) async-start(), calls=%async_computation.19 | async-start | bytes 1310720 | tf_op jit(solution)/shard_map/reduce_scatter | solution.py:264
  2272.1 192.6 %reduce-scatter.17.cloned.1.call-start = ((), (), s32[]{:S(2)}) async-start(), calls=%async_computation.20 | async-start | bytes 1310720 | tf_op jit(solution)/shard_map/reduce_scatter | solution.py:270
  2272.9 193.7 %reduce-scatter.25.cloned.1.call-start = ((), (), s32[]{:S(2)}) async-start(), calls=%async_computation.24 | async-start | bytes 3276800 | tf_op jit(solution)/shard_map/reduce_scatter | solution.py:285
  2277.4 196.8 %reduce-scatter.21.cloned.1.call-start = ((), (), s32[]{:S(2)}) async-start(), calls=%async_computation.22 | async-start | bytes 3276800 | tf_op jit(solution)/shard_map/reduce_scatter | solution.py:279
  2284.9 231.9 %reduce-scatter.23.cloned.1.call-start = ((), (), s32[]{:S(2)}) async-start(), calls=%async_computation.23 | async-start | bytes 3276800 | tf_op jit(solution)/shard_map/reduce_scatter | solution.py:282
  (118 other events, 2799.4 us)
Sparse Core Ops, SparseCore 0:
  9.8 29.2 all-gather.16
  40.9 26.4 all-gather.18
  69.3 26.4 all-gather.20
  97.5 39.4 all-gather.26
  138.8 39.4 all-gather.28
  180.0 26.3 all-gather.22
  208.2 39.3 all-gather.24
  258.9 46.8 all-gather.30
  337.0 88.3 reduce-scatter.26
  428.0 45.3 all-gather.32
  475.5 45.6 all-gather.34
  543.6 88.3 reduce-scatter.28
  636.9 45.3 all-gather.36
  741.7 88.3 reduce-scatter.30
  832.3 87.9 reduce-scatter.32
  927.3 45.3 all-gather.30
  1003.8 88.3 reduce-scatter.26
  1094.9 45.3 all-gather.32
  1142.4 45.6 all-gather.34
  1210.5 88.3 reduce-scatter.28
  1303.7 45.3 all-gather.36
  1408.6 88.3 reduce-scatter.30
  1499.3 87.9 reduce-scatter.32
  1594.4 45.3 all-gather.30
  1670.8 88.3 reduce-scatter.26
  1761.9 45.3 all-gather.32
  1809.3 45.6 all-gather.34
  1877.3 88.3 reduce-scatter.28
  1970.6 45.3 all-gather.36
  2075.5 88.3 reduce-scatter.30
  2166.1 88.0 reduce-scatter.32
  2267.4 26.3 reduce-scatter.18
  2297.1 27.9 reduce-scatter.12
  2328.6 27.9 reduce-scatter.14
  2360.0 27.9 reduce-scatter.16
  2390.9 40.1 reduce-scatter.24
  2433.9 40.2 reduce-scatter.20
  2477.2 39.5 reduce-scatter.22
where the time goes:
time: 2530 us
  waiting for transfers between devices  1640 us (65%)
  matrix products  548 us (22%)
  other arithmetic  151 us (6%)
  local copies, waits for them, and re-layouts  105 us (4%)
  blocking collectives  57.4 us (2%)
    reduce_scatter x6, waiting for transfers between devices, branch_sum(): lax.psum_scatter(jnp.dot(left_mat, right_mat, preferred_element_type=jnp....  531 us
    reduce_scatter x6, waiting for transfers between devices, input_sum(): lax.psum_scatter(times_transpose(left_mat, right_mat), 'tensor', scatter_...  414 us
    all_gather x6, waiting for transfers between devices, gather_norm(): return lax.all_gather(normed, 'tensor', axis=0, tiled=True)  268 us
    all_gather x6, waiting for transfers between devices, gather_grad(): return lax.all_gather(grad_rows, 'tensor', axis=0, tiled=True)  248 us
    dot_general x12, matrix products, times_transpose(): lax.dot_general(left_mat, right_mat, (((1,), (1,)), ((), ())), preferred_...  96.6 us
    dot_general x16, matrix products, bias_one_block(): jnp.einsum('ibj,ihj->bh', onehot, grad_rows, precision=FULL_PRECISION)  88.6 us
    dot_general x12, matrix products, contract_rows(): lax.dot_general(left_mat, right_mat, (((0,), (0,)), ((), ())), preferred_...  84.3 us
    scatter-add x6, other arithmetic, micro_step(): grad_table.at[row_start:row_start + block_len]  58.8 us
  transfers between devices with their start and end apart: 38, of which 30 were waited for; matrix products, arithmetic and copies ran while one was open for 16% of the time, Pallas kernels for 0%

commit v1 on v0

--- a/solution.py
+++ b/solution.py
@@ -8,6 +8,18 @@
 FULL_PRECISION = lax.Precision.HIGHEST
 
 
+def collect(array, axis, dim):
+    ways, here = (lax.axis_size(axis), lax.axis_index(axis))
+    grown, reach = (array, 1)
+    while reach < ways:
+        theirs = lax.ppermute(grown, axis, [(d, d ^ reach) for d in range(ways)])
+        mine_first = jnp.concatenate([grown, theirs], axis=dim)
+        theirs_first = jnp.concatenate([theirs, grown], axis=dim)
+        grown = jnp.where(here & reach == 0, mine_first, theirs_first)
+        reach = 2 * reach
+    return grown
+
+
 def rms_parts(seq_rows, gain_vec):
     inv_rms = lax.rsqrt(jnp.mean(seq_rows * seq_rows, axis=-1, keepdims=True) + norm_eps)
     plain_rows = seq_rows * inv_rms
@@ -42,7 +54,7 @@
 
 
 def gather_grad(grad_rows):
-    return lax.all_gather(grad_rows, "tensor", axis=0, tiled=True)
+    return collect(grad_rows, "tensor", 0)
 
 
 def branch_sum(left_mat, right_mat):

time: 2530 us -> 2950 us (1.17)
  waiting for transfers between devices: 1640 us -> 2040 us
    ppermute x0 -> x18, waiting for transfers between devices: none -> 791 us  [collect(): theirs = lax.ppermute(grown, axis, [(d, d ^ reach) for d in range(ways)])]
    all_gather x6 -> x0, waiting for transfers between devices: 248 us -> none  [gather_grad(): return lax.all_gather(grad_rows, 'tensor', axis=0, tiled=True)]
    all_gather x6, waiting for transfers between devices: 268 us -> 138 us  [gather_norm(): return lax.all_gather(normed, 'tensor', axis=0, tiled=True)]
  transfers between devices with their start and end apart: 38 -> 50, of which waited for: 30 -> 39; matrix products, arithmetic and copies ran while one was open for 16% -> 15% of each run, Pallas kernels for 0% -> 0%
where the time goes in v1:
time: 2950 us; the launch traced here: 2940 us
  waiting for transfers between devices  2040 us (69%)
  matrix products  529 us (18%)
  other arithmetic  174 us (6%)
  local copies, waits for them, and re-layouts  104 us (4%)
  blocking collectives  57.7 us (2%)
    ppermute x18, waiting for transfers between devices, collect(): theirs = lax.ppermute(grown, axis, [(d, d ^ reach) for d in range(ways)])  791 us
    reduce_scatter x6, waiting for transfers between devices, branch_sum(): lax.psum_scatter(jnp.dot(left_mat, right_mat, preferred_element_type=jnp....  531 us
    reduce_scatter x6, waiting for transfers between devices, input_sum(): lax.psum_scatter(times_transpose(left_mat, right_mat), 'tensor', scatter_...  409 us
    all_gather x6, waiting for transfers between devices, gather_norm(): return lax.all_gather(normed, 'tensor', axis=0, tiled=True)  138 us
    dot_general x12, matrix products, contract_rows(): lax.dot_general(left_mat, right_mat, (((0,), (0,)), ((), ())), preferred_...  88.8 us
    dot_general x16, matrix products, bias_one_block(): jnp.einsum('ibj,ihj->bh', onehot, grad_rows, precision=FULL_PRECISION)  88.6 us
    dot_general x12, matrix products, times_transpose(): lax.dot_general(left_mat, right_mat, (((1,), (1,)), ((), ())), preferred_...  84.6 us
  transfers between devices with their start and end apart: 50, of which 39 were waited for; matrix products, arithmetic and copies ran while one was open for 15% of the time, Pallas kernels for 0%

profile of v1, /device:TPU:0, one launch (start us, length us, event | category | flops | bytes accessed | tf_op | source)
XLA Modules:
  0.0 2938.1 jit_solution(1780639868508370534)
XLA Ops:
  11.9 9.7 all-gather
  21.7 73.3 %while.53 = (s32[]{:T(128)}, f32[16,64,4,1024]{3,2,1,0:T(4,128)}, s32[16,64,1024]{2,1,0:T(8,128)}, f32[32,4]{0,1:T(4,128)S(1)}, s32[]{:T(128)}) while((s32[]{:T(128)}, f32[16,64,4,1024]{3,2,1,0:T(4,128)}, s32[16,64,1024]{2,1,0:T(8,128)}, f32[32,4]{0,1:T(4,128)S(1)}, s32[]{:T(128)}) %tuple.173), condition=%wide.region_1.2_spmd.clone, body=%wide.region_0.1_spmd.clone.sunk | while | flops 102760448 | bytes 1835597 | solution.py:84
  95.1 19.3 copy.64
  117.6 19.4 all-gather.21.cloned.1.call-done
  137.1 41.2 %all-gather.23.cloned.1.call-done = bf16[2048,640]{1,0:T(8,128)(2,1)} async-done(((bf16[512,640]{1,0:T(8,128)(2,1)}), bf16[2048,640]{1,0:T(8,128)(2,1)}) %all-gather.23.cloned.1.call-update) | async-done | bytes 2621456 | tf_op jit(solution)/shard_map/all_gather | solution.py:133
  183.6 22.7 all-gather.17.cloned.1.call-done
  206.4 41.2 %all-gather.19.cloned.1.call-done = bf16[640,2048]{1,0:T(8,128)(2,1)} async-done(((bf16[640,512]{1,0:T(8,128)(2,1)}), bf16[640,2048]{1,0:T(8,128)(2,1)}) %all-gather.19.cloned.1.call-update) | async-done | bytes 2621456 | tf_op jit(solution)/shard_map/all_gather | solution.py:134
  255.5 2420.8 %while.54 = (s32[]{:T(128)}, f32[2048,768]{1,0:T(8,128)}, f32[256,2048]{1,0:T(8,128)}, f32[2048,1280]{1,0:T(8,128)}, f32[640,2048]{1,0:T(8,128)}, /*index=5*/f32...) while((s32[]{:T(128)}, f32[2048,768]{1,0:T(8,128)}, ...), condition=%wide.region_19.20_spmd.clone, body=%wide.region_2.19_spmd.clone.sunk | while | flops 40511991808 | bytes 889028736 | solution.py:269
  258.9 47.0 %all-gather.25.cloned.1.call-done = bf16[1024,2048]{1,0:T(8,128)(2,1)} async-done(((bf16[128,2048]{1,0:T(8,128)(2,1)}), bf16[1024,2048]{1,0:T(8,128)(2,1)}) %all-gather.25.cloned.1.call-update) | async-done | bytes 4194320 | tf_op jit(solution)/shard_map/while/body/eval_jaxpr/all_gather | solution.py:53
  337.6 88.5 %reduce-scatter.27.cloned.1.call-done = f32[128,2048]{1,0:T(8,128)} async-done(((f32[1024,2048]{1,0:T(8,128)}), f32[128,2048]{1,0:T(8,128)}) %reduce-scatter.27.cloned.1.call-update) | async-done | bytes 1048592 | tf_op jit(solution)/shard_map/while/body/eval_jaxpr/reduce_scatter | solution.py:61
  434.4 59.2 %collective-permute-done.1 = bf16[256,2048]{1,0:T(8,128)(2,1)} collective-permute-done((bf16[256,2048]{1,0:T(8,128)(2,1)}, bf16[256,2048]{1,0:T(8,128)(2,1)}, u32[]{:S(2)}, u32[]{:S(2)}) %collective-permute-start.1) | collective-permute-done | bytes 1048608 | tf_op jit(solution)/shard_map/while/body/eval_jaxpr/ppermute | solution.py:15
  507.4 83.2 %collective-permute-done.2 = bf16[512,2048]{1,0:T(8,128)(2,1)} collective-permute-done((bf16[512,2048]{1,0:T(8,128)(2,1)}, bf16[512,2048]{1,0:T(8,128)(2,1)}, u32[]{:S(2)}, u32[]{:S(2)}) %collective-permute-start.2) | collective-permute-done | bytes 2097184 | tf_op jit(solution)/shard_map/while/body/eval_jaxpr/ppermute | solution.py:15
  590.6 9.5 fusion.255
  609.7 88.5 %reduce-scatter.29.cloned.1.call-done = f32[128,2048]{1,0:T(8,128)} async-done(((f32[1024,2048]{1,0:T(8,128)}), f32[128,2048]{1,0:T(8,128)}) %reduce-scatter.29.cloned.1.call-update) | async-done | bytes 1048592 | tf_op jit(solution)/shard_map/while/body/eval_jaxpr/reduce_scatter | solution.py:70
  704.4 25.2 collective-permute-done.4
  731.3 92.0 %collective-permute-done.5 = bf16[512,2048]{1,0:T(8,128)(2,1)S(1)} collective-permute-done((bf16[512,2048]{1,0:T(8,128)(2,1)S(1)}, bf16[512,2048]{1,0:T(8,128)(2,1)S(1)}, u32[]{:S(2)}, u32[]{:S(2)}) %collective-permute-start.5) | collective-permute-done | bytes 2097184 | tf_op jit(solution)/shard_map/while/body/eval_jaxpr/ppermute | solution.py:15
  833.1 10.4 add_dynamic-update-slice_fusion.2
  915.6 52.0 %reduce-scatter.31.cloned.1.call-done = f32[128,2048]{1,0:T(8,128)} async-done(((f32[1024,2048]{1,0:T(8,128)}), f32[128,2048]{1,0:T(8,128)}) %reduce-scatter.31.cloned.1.call-update) | async-done | bytes 1048592 | tf_op jit(solution)/shard_map/while/body/eval_jaxpr/reduce_scatter | solution.py:70
  969.4 88.5 %reduce-scatter.33.cloned.1.call-done = f32[128,2048]{1,0:T(8,128)} async-done(((f32[1024,2048]{1,0:T(8,128)}), f32[128,2048]{1,0:T(8,128)}) %reduce-scatter.33.cloned.1.call-update) | async-done | bytes 1048592 | tf_op jit(solution)/shard_map/while/body/eval_jaxpr/reduce_scatter | solution.py:61
  1064.9 45.4 %all-gather.25.cloned.1.call-done = bf16[1024,2048]{1,0:T(8,128)(2,1)} async-done(((bf16[128,2048]{1,0:T(8,128)(2,1)}), bf16[1024,2048]{1,0:T(8,128)(2,1)}) %all-gather.25.cloned.1.call-update) | async-done | bytes 4194320 | tf_op jit(solution)/shard_map/while/body/eval_jaxpr/all_gather | solution.py:53
  1142.1 88.4 %reduce-scatter.27.cloned.1.call-done = f32[128,2048]{1,0:T(8,128)} async-done(((f32[1024,2048]{1,0:T(8,128)}), f32[128,2048]{1,0:T(8,128)}) %reduce-scatter.27.cloned.1.call-update) | async-done | bytes 1048592 | tf_op jit(solution)/shard_map/while/body/eval_jaxpr/reduce_scatter | solution.py:61
  1238.8 59.2 %collective-permute-done.1 = bf16[256,2048]{1,0:T(8,128)(2,1)} collective-permute-done((bf16[256,2048]{1,0:T(8,128)(2,1)}, bf16[256,2048]{1,0:T(8,128)(2,1)}, u32[]{:S(2)}, u32[]{:S(2)}) %collective-permute-start.1) | collective-permute-done | bytes 1048608 | tf_op jit(solution)/shard_map/while/body/eval_jaxpr/ppermute | solution.py:15
  1311.9 83.2 %collective-permute-done.2 = bf16[512,2048]{1,0:T(8,128)(2,1)} collective-permute-done((bf16[512,2048]{1,0:T(8,128)(2,1)}, bf16[512,2048]{1,0:T(8,128)(2,1)}, u32[]{:S(2)}, u32[]{:S(2)}) %collective-permute-start.2) | collective-permute-done | bytes 2097184 | tf_op jit(solution)/shard_map/while/body/eval_jaxpr/ppermute | solution.py:15
  1414.1 88.5 %reduce-scatter.29.cloned.1.call-done = f32[128,2048]{1,0:T(8,128)} async-done(((f32[1024,2048]{1,0:T(8,128)}), f32[128,2048]{1,0:T(8,128)}) %reduce-scatter.29.cloned.1.call-update) | async-done | bytes 1048592 | tf_op jit(solution)/shard_map/while/body/eval_jaxpr/reduce_scatter | solution.py:70
  1508.9 25.2 collective-permute-done.4
  1535.8 92.0 %collective-permute-done.5 = bf16[512,2048]{1,0:T(8,128)(2,1)S(1)} collective-permute-done((bf16[512,2048]{1,0:T(8,128)(2,1)S(1)}, bf16[512,2048]{1,0:T(8,128)(2,1)S(1)}, u32[]{:S(2)}, u32[]{:S(2)}) %collective-permute-start.5) | collective-permute-done | bytes 2097184 | tf_op jit(solution)/shard_map/while/body/eval_jaxpr/ppermute | solution.py:15
  1637.6 10.4 add_dynamic-update-slice_fusion.2
  1693.1 10.8 select_add_fusion.12
  1704.0 11.5 select_add_fusion.11
  1726.3 45.7 %reduce-scatter.31.cloned.1.call-done = f32[128,2048]{1,0:T(8,128)} async-done(((f32[1024,2048]{1,0:T(8,128)}), f32[128,2048]{1,0:T(8,128)}) %reduce-scatter.31.cloned.1.call-update) | async-done | bytes 1048592 | tf_op jit(solution)/shard_map/while/body/eval_jaxpr/reduce_scatter | solution.py:70
  1773.8 88.5 %reduce-scatter.33.cloned.1.call-done = f32[128,2048]{1,0:T(8,128)} async-done(((f32[1024,2048]{1,0:T(8,128)}), f32[128,2048]{1,0:T(8,128)}) %reduce-scatter.33.cloned.1.call-update) | async-done | bytes 1048592 | tf_op jit(solution)/shard_map/while/body/eval_jaxpr/reduce_scatter | solution.py:61
  1869.4 45.4 %all-gather.25.cloned.1.call-done = bf16[1024,2048]{1,0:T(8,128)(2,1)} async-done(((bf16[128,2048]{1,0:T(8,128)(2,1)}), bf16[1024,2048]{1,0:T(8,128)(2,1)}) %all-gather.25.cloned.1.call-update) | async-done | bytes 4194320 | tf_op jit(solution)/shard_map/while/body/eval_jaxpr/all_gather | solution.py:53
  1946.5 88.4 %reduce-scatter.27.cloned.1.call-done = f32[128,2048]{1,0:T(8,128)} async-done(((f32[1024,2048]{1,0:T(8,128)}), f32[128,2048]{1,0:T(8,128)}) %reduce-scatter.27.cloned.1.call-update) | async-done | bytes 1048592 | tf_op jit(solution)/shard_map/while/body/eval_jaxpr/reduce_scatter | solution.py:61
  2043.3 59.2 %collective-permute-done.1 = bf16[256,2048]{1,0:T(8,128)(2,1)} collective-permute-done((bf16[256,2048]{1,0:T(8,128)(2,1)}, bf16[256,2048]{1,0:T(8,128)(2,1)}, u32[]{:S(2)}, u32[]{:S(2)}) %collective-permute-start.1) | collective-permute-done | bytes 1048608 | tf_op jit(solution)/shard_map/while/body/eval_jaxpr/ppermute | solution.py:15
  2116.3 83.2 %collective-permute-done.2 = bf16[512,2048]{1,0:T(8,128)(2,1)} collective-permute-done((bf16[512,2048]{1,0:T(8,128)(2,1)}, bf16[512,2048]{1,0:T(8,128)(2,1)}, u32[]{:S(2)}, u32[]{:S(2)}) %collective-permute-start.2) | collective-permute-done | bytes 2097184 | tf_op jit(solution)/shard_map/while/body/eval_jaxpr/ppermute | solution.py:15
  2218.6 88.5 %reduce-scatter.29.cloned.1.call-done = f32[128,2048]{1,0:T(8,128)} async-done(((f32[1024,2048]{1,0:T(8,128)}), f32[128,2048]{1,0:T(8,128)}) %reduce-scatter.29.cloned.1.call-update) | async-done | bytes 1048592 | tf_op jit(solution)/shard_map/while/body/eval_jaxpr/reduce_scatter | solution.py:70
  2313.4 25.2 collective-permute-done.4
  2340.3 92.0 %collective-permute-done.5 = bf16[512,2048]{1,0:T(8,128)(2,1)S(1)} collective-permute-done((bf16[512,2048]{1,0:T(8,128)(2,1)S(1)}, bf16[512,2048]{1,0:T(8,128)(2,1)S(1)}, u32[]{:S(2)}, u32[]{:S(2)}) %collective-permute-start.5) | collective-permute-done | bytes 2097184 | tf_op jit(solution)/shard_map/while/body/eval_jaxpr/ppermute | solution.py:15
  2442.1 10.4 add_dynamic-update-slice_fusion.2
  2497.6 10.8 select_add_fusion.12
  2508.5 11.5 select_add_fusion.11
  2530.8 45.7 %reduce-scatter.31.cloned.1.call-done = f32[128,2048]{1,0:T(8,128)} async-done(((f32[1024,2048]{1,0:T(8,128)}), f32[128,2048]{1,0:T(8,128)}) %reduce-scatter.31.cloned.1.call-update) | async-done | bytes 1048592 | tf_op jit(solution)/shard_map/while/body/eval_jaxpr/reduce_scatter | solution.py:70
  2578.3 88.5 %reduce-scatter.33.cloned.1.call-done = f32[128,2048]{1,0:T(8,128)} async-done(((f32[1024,2048]{1,0:T(8,128)}), f32[128,2048]{1,0:T(8,128)}) %reduce-scatter.33.cloned.1.call-update) | async-done | bytes 1048592 | tf_op jit(solution)/shard_map/while/body/eval_jaxpr/reduce_scatter | solution.py:61
  2698.8 20.2 copy.65
  2719.1 104.5 %while.55 = (s32[]{:T(128)}, f32[32,4]{0,1:T(4,128)S(1)}, s32[16,64,1024]{2,1,0:T(8,128)}, f32[16,64,4,1024]{3,2,1,0:T(4,128)}, s32[]{:T(128)}, /*index=5*/s32[]{:T(128)}) while((s32[]{:T(128)}, f32[32,4]{0,1:T(4,128)S(1)}, s32[16,64,1024]{2,1,0:T(8,128)}, f32[16,64,4,1024]{3,2,1,0:T(4,128)}, s32[]{:T(128)}, ...), condition=%wide.region_30.31_spmd.clone, body=%wide.region_29.30_spmd.clone.sunk | while | flops 102760704 | bytes 1836127 | solution.py:106
  2823.6 9.7 all-reduce
  2833.3 38.3 %all-reduce.1 = (f32[2048]{0:T(1024)}, f32[2048]{0:T(1024)}) all-reduce(f32[2048]{0:T(1024)S(1)} %copy-done.27, f32[2048]{0:T(1024)S(1)} %copy-done.24), channel_id=1, replica_groups=mesh['dp'=4,'tensor'=8] {'dp','tensor'}, use_global_device_ids=true, to_apply=%region_20.21 | all-reduce | flops 4096 | bytes 32768 | tf_op jit(solution)/shard_map/psum | solution.py:304
  2888.8 40.4 %reduce-scatter.23.cloned.1.call-done = bf16[512,640]{1,0:T(8,128)(2,1)} async-done(((bf16[2048,640]{1,0:T(8,128)(2,1)}), bf16[512,640]{1,0:T(8,128)(2,1)}) %reduce-scatter.23.cloned.1.call-update) | async-done | bytes 655376 | tf_op jit(solution)/shard_map/reduce_scatter | solution.py:294
  (652 shorter events, 710.6 us)
Async XLA Ops:
  7.2 107.2 %all-gather.11.cloned.1.call-start = ((), (), s32[]{:S(2)}) async-start(), calls=%async_computation.11 | async-start | bytes 1310720 | tf_op jit(solution)/shard_map/all_gather | solution.py:128
  7.9 106.5 %all-gather.13.cloned.1.call-start = ((), (), s32[]{:S(2)}) async-start(), calls=%async_computation.12 | async-start | bytes 1310720 | tf_op jit(solution)/shard_map/all_gather | solution.py:129
  8.7 105.7 %all-gather.15.cloned.1.call-start = ((), (), s32[]{:S(2)}) async-start(), calls=%async_computation.13 | async-start | bytes 1310720 | tf_op jit(solution)/shard_map/all_gather | solution.py:130
  9.4 127.7 %all-gather.21.cloned.1.call-start = ((), (), s32[]{:S(2)}) async-start(), calls=%async_computation.16 | async-start | bytes 3276800 | tf_op jit(solution)/shard_map/all_gather | solution.py:132
  10.0 168.3 %all-gather.23.cloned.1.call-start = ((), (), s32[]{:S(2)}) async-start(), calls=%async_computation.17 | async-start | bytes 3276800 | tf_op jit(solution)/shard_map/all_gather | solution.py:133
  10.6 195.8 %all-gather.17.cloned.1.call-start = ((), (), s32[]{:S(2)}) async-start(), calls=%async_computation.14 | async-start | bytes 1310720 | tf_op jit(solution)/shard_map/all_gather | solution.py:131
  11.1 236.5 %all-gather.19.cloned.1.call-start = ((), (), s32[]{:S(2)}) async-start(), calls=%async_computation.15 | async-start | bytes 3276800 | tf_op jit(solution)/shard_map/all_gather | solution.py:134
  255.5 50.3 %all-gather.25.cloned.1.call-start = ((), (), s32[]{:S(2)}) async-start(), calls=%async_computation.25 | async-start | bytes 4718592 | tf_op jit(solution)/shard_map/while/body/eval_jaxpr/all_gather | solution.py:53
  258.8 167.2 %reduce-scatter.27.cloned.1.call-start = ((), (), s32[]{:S(2)}) async-start(), calls=%async_computation.26 | async-start | bytes 9437184 | tf_op jit(solution)/shard_map/while/body/eval_jaxpr/reduce_scatter | solution.py:61
  337.5 160.7 %all-gather.27.cloned.1.call-start = ((), (), s32[]{:S(2)}) async-start(), calls=%async_computation.27 | async-start | bytes 4718592 | tf_op jit(solution)/shard_map/while/body/eval_jaxpr/all_gather | solution.py:53
  428.6 269.6 %reduce-scatter.29.cloned.1.call-start = ((), (), s32[]{:S(2)}) async-start(), calls=%async_computation.28 | async-start | bytes 9437184 | tf_op jit(solution)/shard_map/while/body/eval_jaxpr/reduce_scatter | solution.py:70
  429.7 2.1 collective-permute-start
  434.4 59.2 %collective-permute-start.1 = (bf16[256,2048]{1,0:T(8,128)(2,1)}, bf16[256,2048]{1,0:T(8,128)(2,1)}, u32[]{:S(2)}, u32[]{:S(2)}) collective-permute-start(bf16[256,2048]{1,0:T(8,128)(2,1)} %maximum_select_fusion.20), channel_id=1, source_target_pairs={{0,2},{1,3},{2,0},{3,1},{4,6},{5,7},{6,4},{7,5},{8,10},{9,11},{10,... | collective-permute-start | bytes 3145736 | tf_op jit(solution)/shard_map/while/body/eval_jaxpr/ppermute | solution.py:15
  498.2 92.4 %collective-permute-start.2 = (bf16[512,2048]{1,0:T(8,128)(2,1)}, bf16[512,2048]{1,0:T(8,128)(2,1)}, u32[]{:S(2)}, u32[]{:S(2)}) collective-permute-start(bf16[512,2048]{1,0:T(8,128)(2,1)} %maximum_select_fusion.21), channel_id=1, source_target_pairs={{0,4},{1,5},{2,6},{3,7},{4,0},{5,1},{6,2},{7,3},{8,12},{9,13},{10,... | collective-permute-start | bytes 6291464 | tf_op jit(solution)/shard_map/while/body/eval_jaxpr/ppermute | solution.py:15
  609.5 358.1 %reduce-scatter.31.cloned.1.call-start = ((), (), s32[]{:S(2)}) async-start(), calls=%async_computation.29 | async-start | bytes 9437184 | tf_op jit(solution)/shard_map/while/body/eval_jaxpr/reduce_scatter | solution.py:70
  704.4 25.3 collective-permute-start.4
  730.6 92.7 %collective-permute-start.5 = (bf16[512,2048]{1,0:T(8,128)(2,1)S(1)}, bf16[512,2048]{1,0:T(8,128)(2,1)S(1)}, u32[]{:S(2)}, u32[]{:S(2)}) collective-permute-start(bf16[512,2048]{1,0:T(8,128)(2,1)S(1)} %maximum_select_fusion.23), channel_id=1, source_target_pairs={{0,4},{1,5},{2,6},{3,7},{4,0},{5,1},{6,2},{7,3},{8,12},{9,13},{10,... | collective-permute-start | bytes 6291464 | tf_op jit(solution)/shard_map/while/body/eval_jaxpr/ppermute | solution.py:15
  879.4 178.5 %reduce-scatter.33.cloned.1.call-start = ((), (), s32[]{:S(2)}) async-start(), calls=%async_computation.30 | async-start | bytes 9437184 | tf_op jit(solution)/shard_map/while/body/eval_jaxpr/reduce_scatter | solution.py:61
  1061.5 48.8 %all-gather.25.cloned.1.call-start = ((), (), s32[]{:S(2)}) async-start(), calls=%async_computation.25 | async-start | bytes 4718592 | tf_op jit(solution)/shard_map/while/body/eval_jaxpr/all_gather | solution.py:53
  1064.8 165.6 %reduce-scatter.27.cloned.1.call-start = ((), (), s32[]{:S(2)}) async-start(), calls=%async_computation.26 | async-start | bytes 9437184 | tf_op jit(solution)/shard_map/while/body/eval_jaxpr/reduce_scatter | solution.py:61
  1142.0 160.7 %all-gather.27.cloned.1.call-start = ((), (), s32[]{:S(2)}) async-start(), calls=%async_computation.27 | async-start | bytes 4718592 | tf_op jit(solution)/shard_map/while/body/eval_jaxpr/all_gather | solution.py:53
  1233.0 269.6 %reduce-scatter.29.cloned.1.call-start = ((), (), s32[]{:S(2)}) async-start(), calls=%async_computation.28 | async-start | bytes 9437184 | tf_op jit(solution)/shard_map/while/body/eval_jaxpr/reduce_scatter | solution.py:70
  1234.2 2.1 collective-permute-start
  1238.8 59.2 %collective-permute-start.1 = (bf16[256,2048]{1,0:T(8,128)(2,1)}, bf16[256,2048]{1,0:T(8,128)(2,1)}, u32[]{:S(2)}, u32[]{:S(2)}) collective-permute-start(bf16[256,2048]{1,0:T(8,128)(2,1)} %maximum_select_fusion.20), channel_id=1, source_target_pairs={{0,2},{1,3},{2,0},{3,1},{4,6},{5,7},{6,4},{7,5},{8,10},{9,11},{10,... | collective-permute-start | bytes 3145736 | tf_op jit(solution)/shard_map/while/body/eval_jaxpr/ppermute | solution.py:15
  1302.7 92.4 %collective-permute-start.2 = (bf16[512,2048]{1,0:T(8,128)(2,1)}, bf16[512,2048]{1,0:T(8,128)(2,1)}, u32[]{:S(2)}, u32[]{:S(2)}) collective-permute-start(bf16[512,2048]{1,0:T(8,128)(2,1)} %maximum_select_fusion.21), channel_id=1, source_target_pairs={{0,4},{1,5},{2,6},{3,7},{4,0},{5,1},{6,2},{7,3},{8,12},{9,13},{10,... | collective-permute-start | bytes 6291464 | tf_op jit(solution)/shard_map/while/body/eval_jaxpr/ppermute | solution.py:15
  1413.9 358.1 %reduce-scatter.31.cloned.1.call-start = ((), (), s32[]{:S(2)}) async-start(), calls=%async_computation.29 | async-start | bytes 9437184 | tf_op jit(solution)/shard_map/while/body/eval_jaxpr/reduce_scatter | solution.py:70
  1506.6 2.0 collective-permute-start.3
  1508.8 25.3 collective-permute-start.4
  1535.1 92.7 %collective-permute-start.5 = (bf16[512,2048]{1,0:T(8,128)(2,1)S(1)}, bf16[512,2048]{1,0:T(8,128)(2,1)S(1)}, u32[]{:S(2)}, u32[]{:S(2)}) collective-permute-start(bf16[512,2048]{1,0:T(8,128)(2,1)S(1)} %maximum_select_fusion.23), channel_id=1, source_target_pairs={{0,4},{1,5},{2,6},{3,7},{4,0},{5,1},{6,2},{7,3},{8,12},{9,13},{10,... | collective-permute-start | bytes 6291464 | tf_op jit(solution)/shard_map/while/body/eval_jaxpr/ppermute | solution.py:15
  1683.9 178.5 %reduce-scatter.33.cloned.1.call-start = ((), (), s32[]{:S(2)}) async-start(), calls=%async_computation.30 | async-start | bytes 9437184 | tf_op jit(solution)/shard_map/while/body/eval_jaxpr/reduce_scatter | solution.py:61
  1865.9 48.8 %all-gather.25.cloned.1.call-start = ((), (), s32[]{:S(2)}) async-start(), calls=%async_computation.25 | async-start | bytes 4718592 | tf_op jit(solution)/shard_map/while/body/eval_jaxpr/all_gather | solution.py:53
  1869.3 165.6 %reduce-scatter.27.cloned.1.call-start = ((), (), s32[]{:S(2)}) async-start(), calls=%async_computation.26 | async-start | bytes 9437184 | tf_op jit(solution)/shard_map/while/body/eval_jaxpr/reduce_scatter | solution.py:61
  1946.5 160.7 %all-gather.27.cloned.1.call-start = ((), (), s32[]{:S(2)}) async-start(), calls=%async_computation.27 | async-start | bytes 4718592 | tf_op jit(solution)/shard_map/while/body/eval_jaxpr/all_gather | solution.py:53
  2037.5 269.6 %reduce-scatter.29.cloned.1.call-start = ((), (), s32[]{:S(2)}) async-start(), calls=%async_computation.28 | async-start | bytes 9437184 | tf_op jit(solution)/shard_map/while/body/eval_jaxpr/reduce_scatter | solution.py:70
  2038.7 2.1 collective-permute-start
  2043.3 59.2 %collective-permute-start.1 = (bf16[256,2048]{1,0:T(8,128)(2,1)}, bf16[256,2048]{1,0:T(8,128)(2,1)}, u32[]{:S(2)}, u32[]{:S(2)}) collective-permute-start(bf16[256,2048]{1,0:T(8,128)(2,1)} %maximum_select_fusion.20), channel_id=1, source_target_pairs={{0,2},{1,3},{2,0},{3,1},{4,6},{5,7},{6,4},{7,5},{8,10},{9,11},{10,... | collective-permute-start | bytes 3145736 | tf_op jit(solution)/shard_map/while/body/eval_jaxpr/ppermute | solution.py:15
  2107.1 92.4 %collective-permute-start.2 = (bf16[512,2048]{1,0:T(8,128)(2,1)}, bf16[512,2048]{1,0:T(8,128)(2,1)}, u32[]{:S(2)}, u32[]{:S(2)}) collective-permute-start(bf16[512,2048]{1,0:T(8,128)(2,1)} %maximum_select_fusion.21), channel_id=1, source_target_pairs={{0,4},{1,5},{2,6},{3,7},{4,0},{5,1},{6,2},{7,3},{8,12},{9,13},{10,... | collective-permute-start | bytes 6291464 | tf_op jit(solution)/shard_map/while/body/eval_jaxpr/ppermute | solution.py:15
  2218.4 358.1 %reduce-scatter.31.cloned.1.call-start = ((), (), s32[]{:S(2)}) async-start(), calls=%async_computation.29 | async-start | bytes 9437184 | tf_op jit(solution)/shard_map/while/body/eval_jaxpr/reduce_scatter | solution.py:70
  2313.3 25.3 collective-permute-start.4
  2339.6 92.7 %collective-permute-start.5 = (bf16[512,2048]{1,0:T(8,128)(2,1)S(1)}, bf16[512,2048]{1,0:T(8,128)(2,1)S(1)}, u32[]{:S(2)}, u32[]{:S(2)}) collective-permute-start(bf16[512,2048]{1,0:T(8,128)(2,1)S(1)} %maximum_select_fusion.23), channel_id=1, source_target_pairs={{0,4},{1,5},{2,6},{3,7},{4,0},{5,1},{6,2},{7,3},{8,12},{9,13},{10,... | collective-permute-start | bytes 6291464 | tf_op jit(solution)/shard_map/while/body/eval_jaxpr/ppermute | solution.py:15
  2488.4 178.5 %reduce-scatter.33.cloned.1.call-start = ((), (), s32[]{:S(2)}) async-start(), calls=%async_computation.30 | async-start | bytes 9437184 | tf_op jit(solution)/shard_map/while/body/eval_jaxpr/reduce_scatter | solution.py:61
  2676.3 195.9 %reduce-scatter.19.cloned.1.call-start = ((), (), s32[]{:S(2)}) async-start(), calls=%async_computation.21 | async-start | bytes 1310720 | tf_op jit(solution)/shard_map/reduce_scatter | solution.py:288
  2679.2 194.9 %reduce-scatter.13.cloned.1.call-start = ((), (), s32[]{:S(2)}) async-start(), calls=%async_computation.18 | async-start | bytes 1310720 | tf_op jit(solution)/shard_map/reduce_scatter | solution.py:273
  2684.1 191.8 %reduce-scatter.15.cloned.1.call-start = ((), (), s32[]{:S(2)}) async-start(), calls=%async_computation.19 | async-start | bytes 1310720 | tf_op jit(solution)/shard_map/reduce_scatter | solution.py:276
  2684.8 192.9 %reduce-scatter.17.cloned.1.call-start = ((), (), s32[]{:S(2)}) async-start(), calls=%async_computation.20 | async-start | bytes 1310720 | tf_op jit(solution)/shard_map/reduce_scatter | solution.py:282
  2685.5 193.9 %reduce-scatter.25.cloned.1.call-start = ((), (), s32[]{:S(2)}) async-start(), calls=%async_computation.24 | async-start | bytes 3276800 | tf_op jit(solution)/shard_map/reduce_scatter | solution.py:297
  2690.0 196.5 %reduce-scatter.21.cloned.1.call-start = ((), (), s32[]{:S(2)}) async-start(), calls=%async_computation.22 | async-start | bytes 3276800 | tf_op jit(solution)/shard_map/reduce_scatter | solution.py:291
  2697.5 231.7 %reduce-scatter.23.cloned.1.call-start = ((), (), s32[]{:S(2)}) async-start(), calls=%async_computation.23 | async-start | bytes 3276800 | tf_op jit(solution)/shard_map/reduce_scatter | solution.py:294
  (148 other events, 6003.0 us)
Sparse Core Ops, SparseCore 0:
  9.8 29.2 all-gather.10
  40.9 26.4 all-gather.12
  69.3 26.4 all-gather.14
  97.5 39.4 all-gather.20
  138.8 39.4 all-gather.22
  180.0 26.3 all-gather.16
  208.2 39.3 all-gather.18
  258.9 46.8 all-gather.24
  337.6 88.3 reduce-scatter.26
  428.7 62.7 all-gather.26
  609.6 88.5 reduce-scatter.28
  879.5 88.0 reduce-scatter.30
  969.9 87.9 reduce-scatter.32
  1065.0 45.3 all-gather.24
  1142.1 88.3 reduce-scatter.26
  1233.2 62.7 all-gather.26
  1414.0 88.5 reduce-scatter.28
  1684.0 87.9 reduce-scatter.30
  1774.3 87.9 reduce-scatter.32
  1869.4 45.3 all-gather.24
  1946.6 88.3 reduce-scatter.26
  2037.6 62.7 all-gather.26
  2218.5 88.5 reduce-scatter.28
  2488.5 87.9 reduce-scatter.30
  2578.8 87.9 reduce-scatter.32
  2679.7 26.3 reduce-scatter.18
  2709.5 27.9 reduce-scatter.12
  2740.9 27.9 reduce-scatter.14
  2772.3 27.9 reduce-scatter.16
  2803.2 40.1 reduce-scatter.24
  2846.3 40.1 reduce-scatter.20
  2889.5 39.5 reduce-scatter.22
